TPU v7x, 256 devices: a whole 4x4x8 slice. The times are simulated.
256 devices in a mesh: seq: 16 (over z, core), head: 16 (over y, x).
Axes of the slice: x: 4, y: 4, z: 8, core: 2. Of those that a mesh axis runs over, the one named last changes fastest.
Arguments:
- queries: bfloat16 [6144, 16384], P('seq', 'head'), may hold values from -5 to 5
- keys: bfloat16 [6144, 1024], P('seq', 'head'), may hold values from -5 to 5
- values: bfloat16 [6144, 1024], P('seq', 'head'), may hold values from -6 to 6
- feat_q: bfloat16 [128, 128, 128], P('head'), may hold values from -0.5 to 0.5
- feat_k: bfloat16 [128, 128, 128], P('head'), may hold values from -0.5 to 0.5
Outputs:
- grad_feat_q: float32 [128, 128, 128], P('head')
- grad_feat_k: float32 [128, 128, 128], P('head')
All inputs are finite; a program needn't handle non-finite values.
Results may differ from a plain program's by a relative error of at most 0.02.
Values may be sent and summed in bfloat16 or wider, within the bound.
A program may use at most 128 MiB of HBM per device.

v0:
```python
import math
import jax
import jax.numpy as jnp
from jax import lax
from jax.sharding import PartitionSpec as P

HIGHEST_MODE = lax.Precision.HIGHEST
MASKED_SCORE = -1e30


def from_partner(block, axis, stride):
    count = lax.axis_size(axis)
    route = []
    for low in range(count):
        high = low | 1 << stride
        if high != low and high < count:
            route += [(low, high), (high, low)]
    return lax.ppermute(block, axis, route)


def in_one_piece(arrays, axis, dim, along):
    columns = [a.reshape(*a.shape[:along], -1) for a in arrays]
    both = jnp.concatenate(columns, axis=along)
    filled, at, done = (lax.all_gather(both, axis, axis=dim, tiled=True), 0, [])
    for a, column in zip(arrays, columns):
        piece = filled[..., at : at + column.shape[along]]
        done.append(piece.reshape(*piece.shape[:along], *a.shape[along:]))
        at += column.shape[along]
    return tuple(done)


def together(arrays, axis):
    vector, at, done = (jnp.concatenate([a.reshape(-1) for a in arrays]), 0, [])
    so_far = lax.psum(vector, axis)
    for a in arrays:
        done.append(so_far[at : at + a.size].reshape(a.shape))
        at += a.size
    return tuple(done)


def split_wide(entries):
    high = entries.astype(jnp.bfloat16)
    low = (entries - high.astype(jnp.float32)).astype(jnp.bfloat16)
    return (high, low)


def wide_left(form, wide, narrow):
    high, low = split_wide(wide)
    return jnp.einsum(form, high, narrow, preferred_element_type=jnp.float32) + jnp.einsum(
        form, low, narrow, preferred_element_type=jnp.float32
    )


def wide_right(form, narrow, wide):
    high, low = split_wide(wide)
    return jnp.einsum(form, narrow, high, preferred_element_type=jnp.float32) + jnp.einsum(
        form, narrow, low, preferred_element_type=jnp.float32
    )


def attend_block(
    running, query_half, query_pos, key_rows, value_rows, key_first, group_count, score_scale
):
    row_peak, row_total, summed = running
    half_rows = query_half.shape[0]
    key_count = key_rows.shape[0]
    head_dim = key_rows.shape[1] // group_count
    grouped = query_half.reshape(half_rows, group_count, -1, head_dim)
    key_heads = key_rows.reshape(key_count, group_count, head_dim)
    value_heads = value_rows.reshape(key_count, group_count, head_dim)
    scores = (
        jnp.einsum("rgjd,kgd->gjrk", grouped, key_heads, preferred_element_type=jnp.float32)
        * score_scale
    )
    scores = scores.reshape(row_peak.shape[0], half_rows, key_count)
    key_pos = key_first + jnp.arange(key_count, dtype=jnp.int32)
    allowed = (key_pos[None, :] <= query_pos[:, None])[None]
    new_peak = jnp.maximum(row_peak, jnp.max(jnp.where(allowed, scores, MASKED_SCORE), axis=-1))
    weights = jnp.exp(jnp.where(allowed, scores - new_peak[..., None], MASKED_SCORE))
    factor = jnp.exp(row_peak - new_peak)
    row_total = row_total * factor + jnp.sum(weights, axis=-1)
    rounded = weights.astype(jnp.bfloat16).reshape(group_count, -1, half_rows, key_count)
    mixture = jnp.einsum("gjrk,kgd->gjrd", rounded, value_heads, preferred_element_type=jnp.float32)
    summed = summed * factor[..., None] + mixture.reshape(summed.shape)
    return (new_peak, row_total, summed)


def body(queries, keys, values, feat_q, feat_k):
    row_count = queries.shape[0]
    heads_here = feat_q.shape[0]
    head_dim = feat_q.shape[1]
    seq_count = lax.axis_size("seq")
    seq_place = lax.axis_index("seq")
    head_place = lax.axis_index("head")
    key_value = jnp.stack((keys, values))
    partner = from_partner(key_value, "head", 0)
    upper_half = head_place // (1 << 0) % 2 == 1
    key_value = jnp.where(
        upper_half,
        jnp.concatenate((partner, key_value), axis=2),
        jnp.concatenate((key_value, partner), axis=2),
    )
    group_count = key_value.shape[2] // head_dim
    group_size = heads_here // group_count
    query_pos = seq_place * row_count + jnp.arange(row_count, dtype=jnp.int32)
    half_rows = row_count // 2
    query_halves = (queries[:half_rows], queries[half_rows:])
    pos_halves = (query_pos[:half_rows], query_pos[half_rows:])
    top_halves = (jnp.max(pos_halves[0]), jnp.max(pos_halves[1]))
    score_scale = head_dim ** (-0.5)
    start_half = (
        jnp.full((heads_here, half_rows), MASKED_SCORE, jnp.float32),
        jnp.zeros((heads_here, half_rows), jnp.float32),
        jnp.zeros((heads_here, half_rows, head_dim), jnp.float32),
    )
    shard_part = lax.all_gather(key_value, "seq", axis=1, tiled=True)
    part_rows = shard_part.shape[1]
    block_rows = math.gcd(part_rows, 512)

    def one_step(step_index, halves_state):
        offset = step_index * block_rows
        key_rows = lax.dynamic_slice_in_dim(shard_part[0], offset, block_rows, 0)
        value_rows = lax.dynamic_slice_in_dim(shard_part[1], offset, block_rows, 0)
        updated = []
        for half_index in range(2):

            def attend_half(current, half_index=half_index):
                return attend_block(
                    current,
                    query_halves[half_index],
                    pos_halves[half_index],
                    key_rows,
                    value_rows,
                    offset,
                    group_count,
                    score_scale,
                )

            def unchanged(current):
                return current

            updated.append(
                lax.cond(
                    top_halves[half_index] >= offset,
                    attend_half,
                    unchanged,
                    halves_state[half_index],
                )
            )
        return tuple(updated)

    finished = lax.fori_loop(0, part_rows // block_rows, one_step, (start_half, start_half))
    teacher_out = jnp.concatenate(
        [
            (finished[half_index][2] / finished[half_index][1][..., None]).astype(jnp.bfloat16)
            for half_index in range(2)
        ],
        axis=1,
    )
    key_local = key_value[0].reshape(row_count, group_count, head_dim)
    value_local = key_value[1].reshape(row_count, group_count, head_dim)
    query_local = queries.reshape(row_count, heads_here, head_dim)
    query_pre = jnp.einsum("rhd,hdf->hrf", query_local, feat_q, preferred_element_type=jnp.float32)
    key_pre = jnp.einsum(
        "rgd,gjdf->gjrf",
        key_local,
        feat_k.reshape(group_count, group_size, head_dim, -1),
        preferred_element_type=jnp.float32,
    ).reshape(heads_here, row_count, -1)
    feat_count = query_pre.shape[-1]
    query_feat = jax.nn.softplus(query_pre).astype(jnp.bfloat16)
    key_feat = jax.nn.softplus(key_pre).astype(jnp.bfloat16)
    block_state = jnp.einsum(
        "gjrf,rgd->gjfd",
        key_feat.reshape(group_count, group_size, row_count, -1),
        value_local,
        preferred_element_type=jnp.float32,
    ).reshape(heads_here, feat_count, head_dim)
    block_norm = jnp.sum(key_feat, axis=1, dtype=jnp.float32)
    zero_pair = (jnp.zeros_like(block_state), jnp.zeros_like(block_norm))
    take_shard_part = tuple(
        (
            part.astype(jnp.float32)
            for part in in_one_piece(
                (block_state[None].astype(jnp.bfloat16), block_norm[None].astype(jnp.bfloat16)),
                "seq",
                0,
                3,
            )
        )
    )
    part_count = take_shard_part[0].shape[0]
    chosen = jnp.arange(part_count, dtype=jnp.int32) < seq_place
    before_state = zero_pair[0] + jnp.sum(
        jnp.where(chosen[:, None, None, None], take_shard_part[0], 0.0), axis=0
    )
    before_norm = zero_pair[1] + jnp.sum(
        jnp.where(chosen[:, None, None], take_shard_part[1], 0.0), axis=0
    )
    causal = jnp.arange(row_count)[:, None] >= jnp.arange(row_count)[None, :]
    affinity = jnp.einsum("hrf,hsf->hrs", query_feat, key_feat, preferred_element_type=jnp.float32)
    masked = jnp.where(causal[None], affinity, 0.0)
    local_mix = jnp.einsum(
        "gjrs,sgd->gjrd",
        masked.astype(jnp.bfloat16).reshape(group_count, group_size, row_count, row_count),
        value_local,
        preferred_element_type=jnp.float32,
    ).reshape(heads_here, row_count, head_dim)
    numerator = wide_right("hrf,hfd->hrd", query_feat, before_state) + local_mix
    denominator = wide_right("hrf,hf->hr", query_feat, before_norm) + jnp.sum(masked, axis=-1)
    student = numerator / denominator[..., None]
    total_tokens = row_count * seq_count
    grad_out = 2.0 * (student - teacher_out.astype(jnp.float32)) / total_tokens
    grad_numer = grad_out / denominator[..., None]
    grad_denom = -jnp.sum(grad_out * student, axis=-1) / denominator
    back_state = wide_right("hrf,hrd->hfd", query_feat, grad_numer)
    back_norm = wide_right("hrf,hr->hf", query_feat, grad_denom)

    def take_upper(running, shard_part):
        part_count = shard_part[0].shape[0]
        chosen = jnp.arange(part_count, dtype=jnp.int32) > seq_place
        return (
            running[0]
            + jnp.sum(jnp.where(chosen[:, None, None, None], shard_part[0], 0.0), axis=0),
            running[1] + jnp.sum(jnp.where(chosen[:, None, None], shard_part[1], 0.0), axis=0),
        )

    after_state, after_norm = take_upper(
        zero_pair,
        (
            lax.all_gather(back_state[None].astype(jnp.bfloat16), "seq", axis=0, tiled=True).astype(
                jnp.float32
            ),
            lax.all_gather(back_norm[None].astype(jnp.bfloat16), "seq", axis=0, tiled=True).astype(
                jnp.float32
            ),
        ),
    )
    grad_aff = wide_left(
        "gjrd,sgd->gjrs",
        grad_numer.reshape(group_count, group_size, row_count, head_dim),
        value_local,
    ).reshape(heads_here, row_count, row_count)
    grad_aff = jnp.where(causal[None], grad_aff + grad_denom[..., None], 0.0)
    grad_qfeat = (
        jnp.einsum("hrd,hfd->hrf", grad_numer, before_state, precision=HIGHEST_MODE)
        + grad_denom[..., None] * before_norm[:, None, :]
        + wide_left("hrs,hsf->hrf", grad_aff, key_feat)
    )
    grad_kfeat = (
        wide_right(
            "sgd,gjfd->gjsf",
            value_local,
            after_state.reshape(group_count, group_size, feat_count, head_dim),
        ).reshape(heads_here, row_count, feat_count)
        + after_norm[:, None, :]
        + wide_left("hrs,hrf->hsf", grad_aff, query_feat)
    )
    grad_wq = wide_right("rhd,hrf->hdf", query_local, grad_qfeat * jax.nn.sigmoid(query_pre))
    grad_wk = wide_right(
        "rgd,gjrf->gjdf",
        key_local,
        (grad_kfeat * jax.nn.sigmoid(key_pre)).reshape(
            group_count, group_size, row_count, feat_count
        ),
    ).reshape(heads_here, head_dim, feat_count)
    return tuple(
        (
            part.astype(jnp.float32)
            for part in together(
                (grad_wq.astype(jnp.bfloat16), grad_wk.astype(jnp.bfloat16)), "seq"
            )
        )
    )


def solution(mesh):
    return jax.shard_map(
        body,
        mesh=mesh,
        in_specs=(
            P("seq", "head"),
            P("seq", "head"),
            P("seq", "head"),
            P("head", None, None),
            P("head", None, None),
        ),
        out_specs=(P("head", None, None), P("head", None, None)),
        check_vma=False,
    )
```

profile of v0, /device:TPU:1, one launch (start us, length us, event | category | flops | bytes accessed | tf_op | source)
XLA Modules:
  0.0 392.3 jit_solution(10411164082974506304)
XLA Ops:
  7.2 1.0 copy.115
  8.2 1.0 copy.116
  9.3 2.1 collective-permute-start
  11.4 3.4 collective-permute-done
  14.7 0.9 maximum_select_fusion
  17.0 0.9 select_convert_fusion.2
  18.1 1.1 fusion.123
  19.3 1.0 fusion.71
  21.4 2.2 select_reduce_fusion.1
  23.7 38.1 %all-gather.8.cloned.1.call-done = bf16[2,6144,128]{2,1,0:T(8,128)(2,1)} async-done(((bf16[2,384,128]{2,1,0:T(8,128)(2,1)}), bf16[2,6144,128]{2,1,0:T(8,128)(2,1)}) %all-gather.8.cloned.1.call-update) | async-done | bytes 3145744 | tf_op jit(solution)/shard_map/all_gather | solution.py:116
  61.9 1.0 broadcast_in_dim.136
  62.8 56.6 %while.23 = (s32[]{:T(128)}, f32[8,192]{1,0:T(8,128)S(1)}, f32[8,192]{1,0:T(8,128)S(1)}, f32[8,192,128]{2,1,0:T(8,128)}, f32[8,192]{1,0:T(8,128)S(1)}, /*index=5...) while((s32[]{:T(128)}, f32[8,192]{1,0:T(8,128)S(1)}, ...), condition=%wide.region_15.16_spmd, body=%wide.region_6.15_spmd.sunk | while | flops 823598080 | bytes 37431328 | solution.py:152
  64.0 2.1 fusion.153
  66.2 4.4 %conditional.4 = ((f32[8,192]{1,0:T(8,128)S(1)}, f32[8,192]{1,0:T(8,128)S(1)}, f32[8,192,128]{2,1,0:T(8,128)})) conditional(s32[]{:T(128)} %convert_element_type.400, (f32[8,192]{1,0:T(8,128)S(1)}, f32[8,192]{1,0:T(8,128)S(1)}, f32[8,192,128]{2,1,0:T(8,128)}) %tuple.74, (s32[]{:T(128)}, s32[192]{0:T(256)S(1)}, bf16[192,1024]{1,0:T(8,128)(2,1)S(1)}, ...), branch_computations={%region_7.7_spmd, %region_8.10_spmd} | conditional | flops 411799040 | bytes 18453340 | solution.py:143
  67.1 1.1 fusion.3
  68.2 1.5 fusion.14
  69.7 0.9 copy-done.13
  70.6 3.5 conditional.5
  71.5 1.1 fusion.27
  72.6 1.5 fusion.38
  75.3 2.1 fusion.153
  77.4 4.4 %conditional.4 = ((f32[8,192]{1,0:T(8,128)S(1)}, f32[8,192]{1,0:T(8,128)S(1)}, f32[8,192,128]{2,1,0:T(8,128)})) conditional(s32[]{:T(128)} %convert_element_type.400, (f32[8,192]{1,0:T(8,128)S(1)}, f32[8,192]{1,0:T(8,128)S(1)}, f32[8,192,128]{2,1,0:T(8,128)}) %tuple.74, (s32[]{:T(128)}, s32[192]{0:T(256)S(1)}, bf16[192,1024]{1,0:T(8,128)(2,1)S(1)}, ...), branch_computations={%region_7.7_spmd, %region_8.10_spmd} | conditional | flops 411799040 | bytes 18453340 | solution.py:143
  78.4 1.1 fusion.3
  79.5 1.4 fusion.14
  81.0 0.9 copy-done.13
  81.9 3.5 conditional.5
  82.8 1.1 fusion.27
  83.9 1.5 fusion.38
  86.6 2.1 fusion.153
  90.0 2.2 fusion.153
  93.5 2.1 fusion.153
  96.9 2.1 fusion.153
  100.3 2.1 fusion.153
  103.7 2.1 fusion.153
  107.1 2.1 fusion.153
  110.5 2.1 fusion.153
  113.9 2.1 fusion.153
  117.3 2.1 fusion.153
  119.5 0.9 copy-done.11
  120.3 1.5 copy.125
  121.8 2.5 copy.124
  124.3 2.4 divide_convert_fusion
  126.7 4.6 %slice.72 = bf16[16,8,128,128]{2,1,3,0:T(8,128)(2,1)} slice(bf16[16,8,128,129]{2,1,3,0:T(8,128)(2,1)} %all-gather.6.cloned.1.call-done), slice={[0:16], [0:8], [0:128], [0:128]} | slice | bytes 8388608 | tf_op jit(solution)/shard_map/slice | solution.py:26
  131.2 6.7 %copy.186 = bf16[16,8,128,128]{3,2,1,0:T(8,128)(2,1)} copy(bf16[16,8,128,128]{2,1,3,0:T(8,128)(2,1)} %slice.72) | data formatting | bytes 8388608
  137.9 3.2 select_reduce_fusion
  142.3 1.1 fusion.100
  144.2 1.1 multiply_reduce_fusion
  145.8 1.2 fusion.69
  147.3 2.8 fusion.128
  150.8 0.9 add_select_fusion
  152.0 0.9 fusion.115
  152.9 1.2 copy-done.2
  154.5 1.7 divide_multiply_fusion
  157.1 0.8 copy.138
  158.5 91.9 %all-gather.1 = bf16[128,128]{1,0:T(8,128)(2,1)S(1)} all-gather(bf16[8,128]{1,0:T(8,128)(2,1)S(1)} %add_convert_fusion), channel_id=3, replica_groups=mesh['seq'=16,'head'=16] {'seq'}, dimensions={0}, use_global_device_ids=true | all-gather | bytes 34816 | tf_op jit(solution)/shard_map/all_gather | solution.py:234
  250.5 4.7 %fusion.117 = f32[8,384,128]{2,1,0:T(8,128)S(1)} fusion(bf16[8,384,128]{2,1,0:T(8,128)(2,1)S(1)} %select_convert_fusion.2, f32[8,384,384]{1,2,0:T(8,128)} %copy-done.2), kind=kOutput, calls=%fused_computation.179 | convolution fusion | flops 306708480 | bytes 7077888 | tf_op jit(solution)/shard_map/hrs,hrf->hsf/dot_general | solution.py:49
  255.2 1.9 fusion.113
  257.2 7.9 %all-gather.10.cloned.1.call-done = bf16[128,128,128]{2,1,0:T(8,128)(2,1)} async-done(((bf16[8,128,128]{2,1,0:T(8,128)(2,1)}), bf16[128,128,128]{2,1,0:T(8,128)(2,1)}) %all-gather.10.cloned.1.call-update) | async-done | bytes 4194320 | tf_op jit(solution)/shard_map/all_gather | solution.py:231
  265.1 3.2 fusion.48
  268.8 1.0 copy-done.7
  269.9 2.1 fusion.55
  274.2 108.8 %all-reduce.2.cloned.1.call-done = bf16[262144]{0:T(1024)(128)(2,1)} async-done(((bf16[262144]{0:T(1024)(128)(2,1)}), bf16[262144]{0:T(1024)(128)(2,1)}) %all-reduce.2.cloned.1.call-update) | async-done | bytes 524304 | tf_op jit(solution)/shard_map/psum | solution.py:34
  383.0 1.1 fusion.127
  384.1 0.8 convert.7
  (149 shorter events, 16.1 us)
Async XLA Ops:
  7.2 10.8 %copy-start = (bf16[8,128,128]{2,1,0:T(8,128)(2,1)S(1)}, bf16[8,128,128]{2,1,0:T(8,128)(2,1)}, u32[]{:S(2)}) copy-start(bf16[8,128,128]{2,1,0:T(8,128)(2,1)} %param.15) | copy-start | bytes 786436
  7.2 9.3 %copy-start.5 = (bf16[384,1024]{1,0:T(8,128)(2,1)S(1)}, bf16[384,1024]{1,0:T(8,128)(2,1)}, u32[]{:S(2)}) copy-start(bf16[384,1024]{1,0:T(8,128)(2,1)} %param.11) | copy-start | bytes 2359300
  7.2 54.6 %all-gather.8.cloned.1.call-start = ((), (), s32[]{:S(2)}) async-start(), calls=%async_computation.1 | async-start | bytes 3342336 | tf_op jit(solution)/shard_map/all_gather | solution.py:116
  8.2 8.3 %copy-start.18 = (bf16[8,128,128]{2,1,0:T(8,128)(2,1)S(1)}, bf16[8,128,128]{2,1,0:T(8,128)(2,1)}, u32[]{:S(2)}) copy-start(bf16[8,128,128]{2,1,0:T(8,128)(2,1)} %param.14) | copy-start | bytes 786436
  9.3 5.5 %collective-permute-start = (bf16[2,384,64]{2,1,0:T(8,128)(2,1)S(1)}, bf16[2,384,64]{2,1,0:T(8,128)(2,1)S(1)}, u32[]{:S(2)}, u32[]{:S(2)}) collective-permute-start(bf16[2,384,64]{2,1,0:T(8,128)(2,1)S(1)} %pad_maximum_fusion.3), channel_id=1, source_target_pairs={{0,1},{1,0},{2,3},{3,2},{4,5},{5,4},{6,7},{7,6},{8,9},{9,8},{10,11... | collective-permute-start | bytes 294920 | tf_op jit(solution)/shard_map/ppermute | solution.py:18
  15.7 111.0 %all-gather.6.cloned.1.call-start = ((), (), s32[]{:S(2)}) async-start(), calls=%async_computation | async-start | bytes 4491264 | tf_op jit(solution)/shard_map/all_gather | solution.py:24
  17.0 2.2 copy-start.3
  17.0 1.1 copy-start.8
  19.2 1.2 copy-start.14
  19.2 2.2 copy-start.9
  21.2 243.9 %all-gather.10.cloned.1.call-start = ((), (), s32[]{:S(2)}) async-start(), calls=%async_computation.3 | async-start | bytes 4456448 | tf_op jit(solution)/shard_map/all_gather | solution.py:231
  67.1 1.1 copy-start.12
  69.7 0.9 copy-start.13
  78.4 1.2 copy-start.12
  81.0 0.9 copy-start.13
  119.5 0.9 copy-start.11
  141.8 2.4 copy-start.19
  142.2 1.9 copy-start.16
  142.3 1.9 copy-start.17
  147.0 236.0 %all-reduce.2.cloned.1.call-start = ((), (), s32[]{:S(2)}) async-start(), calls=%async_computation.2 | async-start | bytes 1048576 | tf_op jit(solution)/shard_map/psum | solution.py:34
  150.8 1.1 copy-start.10
  152.0 2.1 copy-start.2
  152.0 2.5 copy-start.4
  154.5 1.7 copy-start.6
  156.2 99.0 %slice-start = ((s8[4718592]{0:T(1024)(128)(4,1)}), s8[524288]{0:T(1024)(128)(4,1)S(1)}, s32[]{:S(2)}) async-start(s8[4718592]{0:T(1024)(128)(4,1)} %bitcast.271), calls=%async_computation.4 | async-start | bytes 1048576
  158.2 97.0 %slice-start.1 = ((s8[4718592]{0:T(1024)(128)(4,1)}), s8[4194304]{0:T(1024)(128)(4,1)S(1)}, s32[]{:S(2)}) async-start(s8[4718592]{0:T(1024)(128)(4,1)} %bitcast.271), calls=%async_computation.5 | async-start | bytes 8388608
  268.5 1.4 copy-start.7
  272.4 1.0 copy-start.15
  274.2 111.6 %copy-start.1 = (bf16[8,128,128]{2,1,0:T(8,128)(2,1)S(1)}, bf16[8,128,128]{2,1,0:T(8,128)(2,1)}, u32[]{:S(2)}) copy-start(bf16[8,128,128]{2,1,0:T(8,128)(2,1)} %param.15) | copy-start | bytes 786436
Sparse Core Ops, SparseCore 0:
  15.8 45.9 all-gather.7
  63.7 40.6 all-gather.5
  147.1 117.8 all-gather.9
  274.3 108.6 all-reduce.1
where the time goes:
time: 394 us; the launch traced here: 392 us
  waiting for transfers between devices  158 us (40%)
  blocking collectives  91.9 us (23%)
  local copies, waits for them, and re-layouts  53.3 us (14%)
  matrix products  36.4 us (9%)
  other arithmetic  20.1 us (5%)
  loops' own time  15.4 us (4%)
  between operations  14.2 us (4%)
    psum x1, waiting for transfers between devices, together(): so_far = lax.psum(vector, axis)  109 us
    all_gather x1, blocking collectives, body(): lax.all_gather(back_norm[None].astype(jnp.bfloat16), 'seq', axis=0, tiled...  91.9 us
    all_gather x1, waiting for transfers between devices, body(): shard_part = lax.all_gather(key_value, 'seq', axis=1, tiled=True)  38.1 us
    slice x12, local copies, waits for them, and re-layouts, one_step(): value_rows = lax.dynamic_slice_in_dim(shard_part[1], offset, block_rows, 0)  25.2 us
    another operation x1, loops' own time, body(): lax.fori_loop(0, part_rows // block_rows, one_step, (start_half, start_ha...  14.8 us
    unnamed x45, local copies, waits for them, and re-layouts  13.5 us
  transfers between devices with their start and end apart: 5, of which 4 were waited for; matrix products, arithmetic and copies ran while one was open for 18% of the time, Pallas kernels for 0%

commit v1 on v0

--- a/solution.py
+++ b/solution.py
@@ -231,9 +231,15 @@
             lax.all_gather(back_state[None].astype(jnp.bfloat16), "seq", axis=0, tiled=True).astype(
                 jnp.float32
             ),
-            lax.all_gather(back_norm[None].astype(jnp.bfloat16), "seq", axis=0, tiled=True).astype(
-                jnp.float32
-            ),
+            jnp.concatenate(
+                lax.all_to_all(
+                    jnp.stack([back_norm[None].astype(jnp.bfloat16)] * lax.axis_size("seq")),
+                    "seq",
+                    0,
+                    0,
+                ),
+                axis=0,
+            ).astype(jnp.float32),
         ),
     )
     grad_aff = wide_left(

time: 394 us -> 411 us (1.043)
  starting transfers between devices: 2.68 us -> 98.3 us
  blocking collectives: 91.9 us -> 0 us
  waiting for transfers between devices: 158 us -> 171 us
    all_to_all x0 -> x1, starting transfers between devices: none -> 95.9 us  [body(): lax.all_to_all(jnp.stack([back_norm[None].astype(jnp.bfloat16)] * lax.axi...]
    all_gather x1 -> x0, blocking collectives: 91.9 us -> none  [body(): lax.all_gather(back_norm[None].astype(jnp.bfloat16), 'seq', axis=0, tiled...]
    all_gather x1, waiting for transfers between devices: 7.88 us -> 22 us  [body(): lax.all_gather(back_state[None].astype(jnp.bfloat16), 'seq', axis=0, tile...]
    unnamed x45 -> x53, local copies, waits for them, and re-layouts: 13.5 us -> 12.2 us
  transfers between devices with their start and end apart: 5 -> 6, of which waited for: 4 -> 4; matrix products, arithmetic and copies ran while one was open for 18% -> 18% of each run, Pallas kernels for 0% -> 0%
where the time goes in v1:
time: 411 us; the launch traced here: 409 us
  waiting for transfers between devices  171 us (42%)
  starting transfers between devices  98.3 us (24%)
  local copies, waits for them, and re-layouts  52 us (13%)
  matrix products  34.2 us (8%)
  other arithmetic  24 us (6%)
  loops' own time  15.5 us (4%)
  between operations  14.3 us (3%)
    psum x1, waiting for transfers between devices, together(): so_far = lax.psum(vector, axis)  109 us
    all_to_all x1, starting transfers between devices, body(): lax.all_to_all(jnp.stack([back_norm[None].astype(jnp.bfloat16)] * lax.axi...  95.9 us
    all_gather x1, waiting for transfers between devices, body(): shard_part = lax.all_gather(key_value, 'seq', axis=1, tiled=True)  36.4 us
    slice x12, local copies, waits for them, and re-layouts, one_step(): value_rows = lax.dynamic_slice_in_dim(shard_part[1], offset, block_rows, 0)  25.2 us
    all_gather x1, waiting for transfers between devices, body(): lax.all_gather(back_state[None].astype(jnp.bfloat16), 'seq', axis=0, tile...  22 us
    another operation x1, loops' own time, body(): lax.fori_loop(0, part_rows // block_rows, one_step, (start_half, start_ha...  14.9 us
    unnamed x53, local copies, waits for them, and re-layouts  12.2 us
  transfers between devices with their start and end apart: 6, of which 4 were waited for; matrix products, arithmetic and copies ran while one was open for 18% of the time, Pallas kernels for 0%

profile of v1, /device:TPU:1, one launch (start us, length us, event | category | flops | bytes accessed | tf_op | source)
XLA Modules:
  0.0 409.2 jit_solution(2829315681010580472)
XLA Ops:
  7.2 1.0 copy.116
  8.2 1.0 copy.117
  9.3 2.1 collective-permute-start
  11.4 3.4 collective-permute-done
  14.7 0.9 maximum_select_fusion
  16.4 1.3 slice_reduce_fusion
  18.1 0.9 select_convert_fusion.2
  19.3 1.1 fusion.123
  20.4 1.0 fusion.71
  22.6 2.8 select_reduce_fusion.1
  25.4 36.4 %all-gather.7.cloned.1.call-done = bf16[2,6144,128]{2,1,0:T(8,128)(2,1)} async-done(((bf16[2,384,128]{2,1,0:T(8,128)(2,1)}), bf16[2,6144,128]{2,1,0:T(8,128)(2,1)}) %all-gather.7.cloned.1.call-update) | async-done | bytes 3145744 | tf_op jit(solution)/shard_map/all_gather | solution.py:116
  61.9 1.0 broadcast_in_dim.136
  62.9 59.4 %while.23 = (s32[]{:T(128)}, f32[8,192]{1,0:T(8,128)S(1)}, f32[8,192]{1,0:T(8,128)S(1)}, f32[8,192,128]{2,1,0:T(8,128)}, f32[8,192]{1,0:T(8,128)S(1)}, /*index=5...) while((s32[]{:T(128)}, f32[8,192]{1,0:T(8,128)S(1)}, ...), condition=%wide.region_15.16_spmd, body=%wide.region_6.15_spmd.sunk | while | flops 823598080 | bytes 37431328 | solution.py:152
  64.1 2.1 fusion.153
  66.2 5.2 %conditional.4 = ((f32[8,192]{1,0:T(8,128)S(1)}, f32[8,192]{1,0:T(8,128)S(1)}, f32[8,192,128]{2,1,0:T(8,128)})) conditional(s32[]{:T(128)} %convert_element_type.401, (f32[8,192]{1,0:T(8,128)S(1)}, f32[8,192]{1,0:T(8,128)S(1)}, f32[8,192,128]{2,1,0:T(8,128)}) %tuple.74, (s32[]{:T(128)}, s32[192]{0:T(256)}, bf16[192,1024]{1,0:T(8,128)(2,1)S(1)}, ...), branch_computations={%region_7.7_spmd, %region_8.10_spmd} | conditional | flops 411799040 | bytes 18453340 | solution.py:143
  67.8 1.1 fusion.3
  68.9 1.5 fusion.14
  70.4 0.9 copy-done.13
  71.4 4.2 %conditional.5 = ((f32[8,192]{1,0:T(8,128)S(1)}, f32[8,192]{1,0:T(8,128)S(1)}, f32[8,192,128]{2,1,0:T(8,128)S(1)})) conditional(s32[]{:T(128)} %convert_element_type.402, (f32[8,192]{1,0:T(8,128)S(1)}, f32[8,192]{1,0:T(8,128)S(1)}, f32[8,192,128]{2,1,0:T(8,128)S(1)}) %tuple.76, (s32[]{:T(128)}, s32[192]{0:T(256)}, ...), branch_computations={%region_11.11_spmd, %region_12.14_spmd} | conditional | flops 411799040 | bytes 12161828 | solution.py:143
  72.9 1.1 fusion.27
  74.0 1.5 fusion.38
  76.8 2.1 fusion.153
  78.9 5.2 %conditional.4 = ((f32[8,192]{1,0:T(8,128)S(1)}, f32[8,192]{1,0:T(8,128)S(1)}, f32[8,192,128]{2,1,0:T(8,128)})) conditional(s32[]{:T(128)} %convert_element_type.401, (f32[8,192]{1,0:T(8,128)S(1)}, f32[8,192]{1,0:T(8,128)S(1)}, f32[8,192,128]{2,1,0:T(8,128)}) %tuple.74, (s32[]{:T(128)}, s32[192]{0:T(256)}, bf16[192,1024]{1,0:T(8,128)(2,1)S(1)}, ...), branch_computations={%region_7.7_spmd, %region_8.10_spmd} | conditional | flops 411799040 | bytes 18453340 | solution.py:143
  80.5 1.1 fusion.3
  81.7 1.5 fusion.14
  83.2 0.9 copy-done.13
  84.1 4.2 %conditional.5 = ((f32[8,192]{1,0:T(8,128)S(1)}, f32[8,192]{1,0:T(8,128)S(1)}, f32[8,192,128]{2,1,0:T(8,128)S(1)})) conditional(s32[]{:T(128)} %convert_element_type.402, (f32[8,192]{1,0:T(8,128)S(1)}, f32[8,192]{1,0:T(8,128)S(1)}, f32[8,192,128]{2,1,0:T(8,128)S(1)}) %tuple.76, (s32[]{:T(128)}, s32[192]{0:T(256)}, ...), branch_computations={%region_11.11_spmd, %region_12.14_spmd} | conditional | flops 411799040 | bytes 12161828 | solution.py:143
  85.7 1.1 fusion.27
  86.8 1.5 fusion.38
  89.5 2.1 fusion.153
  92.9 2.1 fusion.153
  96.4 2.1 fusion.153
  99.8 2.1 fusion.153
  103.2 2.1 fusion.153
  106.6 2.1 fusion.153
  110.0 2.1 fusion.153
  113.4 2.1 fusion.153
  116.7 2.1 fusion.153
  120.1 2.1 fusion.153
  122.3 0.9 copy-done.11
  123.2 1.5 copy.126
  124.7 2.4 copy.125
  127.1 2.4 divide_convert_fusion
  129.5 4.6 %slice.72 = bf16[16,8,128,128]{2,1,3,0:T(8,128)(2,1)} slice(bf16[16,8,128,129]{2,1,3,0:T(8,128)(2,1)} %all-gather.5.cloned.1.call-done), slice={[0:16], [0:8], [0:128], [0:128]} | slice | bytes 8388608 | tf_op jit(solution)/shard_map/slice | solution.py:26
  134.1 6.8 %copy.188 = bf16[16,8,128,128]{3,2,1,0:T(8,128)(2,1)} copy(bf16[16,8,128,128]{2,1,3,0:T(8,128)(2,1)} %slice.72) | data formatting | bytes 8388608
  140.9 3.2 select_reduce_fusion
  145.4 1.1 fusion.100
  147.4 1.1 multiply_reduce_fusion
  149.0 1.2 fusion.69
  151.4 95.9 %all-to-all-start = ((bf16[16,1,8,128]{3,2,1,0:T(8,128)(2,1)}), bf16[16,1,8,128]{3,2,1,0:T(8,128)(2,1)S(1)}, u32[]{:S(2)}, u32[]{:S(2)}) async-start(bf16[16,1,8,128]{3,2,1,0:T(8,128)(2,1)} %stack.11), calls=%async_computation | async-start | bytes 65536 | tf_op jit(solution)/shard_map/all_to_all | solution.py:235
  247.3 3.8 fusion.128
  251.9 0.9 add_select_fusion
  253.0 0.9 fusion.115
  254.4 1.7 divide_multiply_fusion
  257.4 2.0 fusion.113
  260.1 22.0 %all-gather.9.cloned.1.call-done = bf16[128,128,128]{2,1,0:T(8,128)(2,1)} async-done(((bf16[8,128,128]{2,1,0:T(8,128)(2,1)}), bf16[128,128,128]{2,1,0:T(8,128)(2,1)}) %all-gather.9.cloned.1.call-update) | async-done | bytes 4194320 | tf_op jit(solution)/shard_map/all_gather | solution.py:231
  282.1 3.2 fusion.48
  285.9 1.0 copy-done.5
  286.9 2.1 fusion.55
  290.1 0.8 pad_maximum_fusion.1
  290.9 109.0 %all-reduce.2.cloned.1.call-done = bf16[262144]{0:T(1024)(128)(2,1)} async-done(((bf16[262144]{0:T(1024)(128)(2,1)}), bf16[262144]{0:T(1024)(128)(2,1)}) %all-reduce.2.cloned.1.call-update) | async-done | bytes 524304 | tf_op jit(solution)/shard_map/psum | solution.py:34
  400.0 1.1 fusion.127
  401.1 0.8 convert.8
  401.9 0.8 convert.9
  (158 shorter events, 18.3 us)
Async XLA Ops:
  7.2 11.9 %copy-start = (bf16[8,128,128]{2,1,0:T(8,128)(2,1)S(1)}, bf16[8,128,128]{2,1,0:T(8,128)(2,1)}, u32[]{:S(2)}) copy-start(bf16[8,128,128]{2,1,0:T(8,128)(2,1)} %param.15) | copy-start | bytes 786436
  7.2 10.5 %copy-start.4 = (bf16[384,1024]{1,0:T(8,128)(2,1)S(1)}, bf16[384,1024]{1,0:T(8,128)(2,1)}, u32[]{:S(2)}) copy-start(bf16[384,1024]{1,0:T(8,128)(2,1)} %param.11) | copy-start | bytes 2359300
  7.2 54.6 %all-gather.7.cloned.1.call-start = ((), (), s32[]{:S(2)}) async-start(), calls=%async_computation.2 | async-start | bytes 3342336 | tf_op jit(solution)/shard_map/all_gather | solution.py:116
  8.2 9.5 %copy-start.19 = (bf16[8,128,128]{2,1,0:T(8,128)(2,1)S(1)}, bf16[8,128,128]{2,1,0:T(8,128)(2,1)}, u32[]{:S(2)}) copy-start(bf16[8,128,128]{2,1,0:T(8,128)(2,1)} %param.14) | copy-start | bytes 786436
  9.3 5.5 %collective-permute-start = (bf16[2,384,64]{2,1,0:T(8,128)(2,1)S(1)}, bf16[2,384,64]{2,1,0:T(8,128)(2,1)S(1)}, u32[]{:S(2)}, u32[]{:S(2)}) collective-permute-start(bf16[2,384,64]{2,1,0:T(8,128)(2,1)S(1)} %pad_maximum_fusion.3), channel_id=1, source_target_pairs={{0,1},{1,0},{2,3},{3,2},{4,5},{5,4},{6,7},{7,6},{8,9},{9,8},{10,11... | collective-permute-start | bytes 294920 | tf_op jit(solution)/shard_map/ppermute | solution.py:18
  15.7 113.9 %all-gather.5.cloned.1.call-start = ((), (), s32[]{:S(2)}) async-start(), calls=%async_computation.1 | async-start | bytes 4491264 | tf_op jit(solution)/shard_map/all_gather | solution.py:24
  16.3 6.2 %copy-start.15 = (pred[384,384]{0,1:T(8,128)(4,1)}, pred[384,384]{0,1:T(8,128)(4,1)S(1)}, u32[]{:S(2)}) copy-start(pred[384,384]{0,1:T(8,128)(4,1)S(1)} %iota_compare_fusion) | copy-start | bytes 442372
  18.1 2.2 copy-start.2
  18.1 1.1 copy-start.6
  20.4 1.2 copy-start.14
  20.4 2.2 copy-start.9
  22.3 259.8 %all-gather.9.cloned.1.call-start = ((), (), s32[]{:S(2)}) async-start(), calls=%async_computation.4 | async-start | bytes 4456448 | tf_op jit(solution)/shard_map/all_gather | solution.py:231
  67.8 1.1 copy-start.12
  70.4 0.9 copy-start.13
  80.5 1.2 copy-start.12
  83.2 0.9 copy-start.13
  122.3 0.9 copy-start.11
  134.1 6.8 %copy-start.23 = (pred[16]{0:T(512)(128)(4,1)S(1)}, pred[16]{0:T(512)(128)(4,1)}, u32[]{:S(2)}) copy-start(pred[16]{0:T(512)(128)(4,1)} %iota_compare_fusion.2) | copy-start | bytes 52
  144.1 0.8 copy-start.8
  144.9 2.4 copy-start.22
  144.9 2.4 copy-start.25
  145.4 2.0 copy-start.7
  145.4 2.0 copy-start.16
  145.4 2.0 copy-start.17
  145.4 2.0 copy-start.18
  146.5 2.0 copy-start.20
  150.2 109.8 %copy-start.24 = (pred[16]{0:T(512)(128)(4,1)}, pred[16]{0:T(512)(128)(4,1)S(1)}, u32[]{:S(2)}) copy-start(pred[16]{0:T(512)(128)(4,1)S(1)} %iota_compare_fusion.1) | copy-start | bytes 52
  151.4 108.6 %all-to-all-start = ((bf16[16,1,8,128]{3,2,1,0:T(8,128)(2,1)}), bf16[16,1,8,128]{3,2,1,0:T(8,128)(2,1)S(1)}, u32[]{:S(2)}, u32[]{:S(2)}) async-start(bf16[16,1,8,128]{3,2,1,0:T(8,128)(2,1)} %stack.11), calls=%async_computation | async-start | bytes 65536 | tf_op jit(solution)/shard_map/all_to_all | solution.py:235
  247.3 152.7 %all-reduce.2.cloned.1.call-start = ((), (), s32[]{:S(2)}) async-start(), calls=%async_computation.3 | async-start | bytes 1048576 | tf_op jit(solution)/shard_map/psum | solution.py:34
  251.9 1.1 copy-start.10
  253.0 1.4 copy-start.3
  253.0 1.4 copy-start.21
  285.5 1.4 copy-start.5
  290.9 111.8 %copy-start.1 = (bf16[8,128,128]{2,1,0:T(8,128)(2,1)S(1)}, bf16[8,128,128]{2,1,0:T(8,128)(2,1)}, u32[]{:S(2)}) copy-start(bf16[8,128,128]{2,1,0:T(8,128)(2,1)} %param.15) | copy-start | bytes 786436
Sparse Core Ops, SparseCore 0:
  15.8 45.9 all-gather.6
  63.7 40.6 all-gather.4
  150.3 131.7 all-gather.8
  291.1 108.8 all-reduce.1
